TPU v7x, 512 devices: a whole 4x8x8 slice. The times are simulated.
512 devices in a mesh: grp: 64 (over x, z, core), tp: 8 (over y).
Axes of the slice: x: 4, y: 8, z: 8, core: 2. Of those that a mesh axis runs over, the one named last changes fastest.
Arguments:
- patches: bfloat16 [65536, 1280], P(('grp', 'tp')), may hold values from -6 to 6
- pictures: int32 [64, 1024], P('grp', 'tp'), may hold values from 0 to 1, as said below
- vis_qkv: bfloat16 [3, 1280, 1280], P(None, 'tp'), as said below
- vis_out: bfloat16 [1280, 1280], P(None, 'grp'), may hold values from -0.15625 to 0.15625
- merge_w: bfloat16 [1280, 5120], P('tp'), may hold values from -0.078125 to 0.078125
- text: bfloat16 [65536, 1280], P(('grp', 'tp')), may hold values from -6 to 6
- places: int32 [16384], P(('grp', 'tp')), may hold values from 0 to 65535, as said below
- segments: int32 [64, 1024], P('grp', 'tp'), may hold values from 0 to 3, never falling along the last dimension, each value on 1 to 512 neighbouring positions
- txt_qkv: bfloat16 [3, 1280, 1280], P(None, 'tp'), as said below
- txt_out: bfloat16 [1280, 1280], P(None, 'grp'), may hold values from -0.15625 to 0.15625
Outputs:
- hidden_out: bfloat16 [65536, 1280], P(('grp', 'tp'))
Inputs may be any that keep to these rules, and one draw needn't show every extreme that they name: `pictures`: within each row, picture numbers never fall; each picture is a run of whole aligned blocks of 4 positions and covers at least a quarter of the row, rounded down to whole blocks of 4 (at least one block). Row 0 holds one picture, row 1 two, the others one or two. `places`: all positions are distinct. The image rows of one device (aligned blocks of 32 rows, devices in the order of the placement) go to tokens held by the device of the same tp index in their token group: to 16 different token groups, exactly 2 rows to each. For each tp index, one token group receives 2 rows from every device of that tp index. `vis_qkv`: the query and key parts of a head may be correlated. `txt_qkv`: the query and key parts of a head may be correlated.
All inputs are finite; a program needn't handle non-finite values.
Results may differ from a plain program's by a relative error of at most 0.01.
Values may be sent and summed in bfloat16 or wider, within the bound.
A program may use at most 64 MiB of HBM per device.

v0:
```python
import jax
import jax.numpy as jnp
from jax import lax
from jax.sharding import PartitionSpec as P

HEAD_DIM = 80
SEND_CAP = 2
EPSILON = 1e-05
MASKED = -1e30


def layer_norm(rows):
    widened = rows.astype(jnp.float32)
    row_mean = jnp.mean(widened, axis=-1, keepdims=True)
    centred = widened - row_mean
    spread = jnp.mean(centred * centred, axis=-1, keepdims=True)
    return (centred * lax.rsqrt(spread + EPSILON)).astype(jnp.bfloat16)


def times_transpose(left, right):
    return lax.dot_general(
        left, right, (((1,), (1,)), ((), ())), preferred_element_type=jnp.float32
    )


def local_attention(queries, key_rows, value_rows, labels, causal):
    row_count, col_count = queries.shape
    heads_here = col_count // HEAD_DIM
    q_heads = queries.reshape(row_count, heads_here, HEAD_DIM)
    k_heads = key_rows.reshape(row_count, heads_here, HEAD_DIM)
    v_heads = value_rows.reshape(row_count, heads_here, HEAD_DIM)
    blocks = max(1, min(8, row_count // 512))
    block_rows = row_count // blocks
    inv_root = HEAD_DIM ** (-0.5)
    outputs = []
    for block_index in range(blocks):
        begin_row = block_index * block_rows
        end_key = begin_row + block_rows if causal else row_count
        scores = (
            jnp.einsum(
                "qhd,khd->hqk",
                q_heads[begin_row : begin_row + block_rows],
                k_heads[:end_key],
                preferred_element_type=jnp.float32,
            )
            * inv_root
        )
        allowed = labels[begin_row : begin_row + block_rows, None] == labels[None, :end_key]
        if causal:
            query_ids = jnp.arange(begin_row, begin_row + block_rows, dtype=jnp.int32)
            key_ids = jnp.arange(end_key, dtype=jnp.int32)
            allowed = allowed & (query_ids[:, None] >= key_ids[None, :])
        scores = jnp.where(allowed[None], scores, MASKED)
        row_max = jnp.max(scores, axis=-1, keepdims=True)
        weights = jnp.exp(scores - row_max)
        prob_bf = (weights / jnp.sum(weights, axis=-1, keepdims=True)).astype(jnp.bfloat16)
        mixed = jnp.einsum(
            "hqk,khd->qhd", prob_bf, v_heads[:end_key], preferred_element_type=jnp.float32
        )
        outputs.append(mixed.astype(jnp.bfloat16).reshape(block_rows, col_count))
    return jnp.concatenate(outputs, axis=0)


def attention_heads(gathered, weights, labels, causal):
    queries = times_transpose(gathered, weights[0]).astype(jnp.bfloat16)
    key_rows = times_transpose(gathered, weights[1]).astype(jnp.bfloat16)
    value_rows = times_transpose(gathered, weights[2]).astype(jnp.bfloat16)
    return local_attention(queries, key_rows, value_rows, labels, causal)


def project_out(rows_here, columns):
    return jnp.dot(
        rows_here,
        lax.all_gather(columns, "grp", axis=1, tiled=True),
        preferred_element_type=jnp.float32,
    )


def per_device(
    patches, pictures, vis_qkv, vis_out, merge_w, text, places, segments, txt_qkv, txt_out
):
    tp_count = lax.axis_size("tp")
    grp_count = lax.axis_size("grp")
    patch_normed = layer_norm(patches)
    group_rows, group_pics = (
        lax.all_gather(patch_normed, "tp", axis=0, tiled=True),
        lax.all_gather(pictures, "tp", axis=1, tiled=True),
    )
    heads_vis = attention_heads(group_rows, vis_qkv, group_pics[0], False)
    own_heads = lax.all_to_all(heads_vis, "tp", split_axis=0, concat_axis=1, tiled=True)
    vis_hidden = (patches.astype(jnp.float32) + project_out(own_heads, vis_out)).astype(
        jnp.bfloat16
    )
    merged = layer_norm(vis_hidden).reshape(patches.shape[0] // 4, 4 * patches.shape[1])
    image_cols = times_transpose(lax.all_gather(merged, "tp", axis=0, tiled=True), merge_w).astype(
        jnp.bfloat16
    )
    image_rows = lax.all_to_all(image_cols, "tp", split_axis=0, concat_axis=1, tiled=True)
    tok_count = text.shape[0]
    group_tokens = tok_count * tp_count
    dest_group = places // group_tokens
    dest_local = places % tok_count
    row_total = places.shape[0]
    row_ids = jnp.arange(row_total, dtype=jnp.int32)
    earlier = row_ids[:, None] > row_ids[None, :]
    same_dest = dest_group[:, None] == dest_group[None, :]
    slot_rank = jnp.sum((earlier & same_dest).astype(jnp.int32), axis=1)
    slot_index = dest_group * SEND_CAP + slot_rank
    slot_ids = jnp.arange(grp_count * SEND_CAP, dtype=jnp.int32)
    slot_pick = slot_ids[:, None] == slot_index[None, :]
    send_rows = jnp.dot(
        slot_pick.astype(jnp.bfloat16), image_rows, preferred_element_type=jnp.float32
    ).astype(jnp.bfloat16)
    send_pos = jnp.sum(jnp.where(slot_pick, dest_local[None, :] + 1, 0), axis=1) - 1
    send_rows = send_rows.reshape(grp_count, SEND_CAP, image_rows.shape[1])
    send_pos = send_pos.reshape(grp_count, SEND_CAP)
    recv_rows, recv_pos = (
        lax.all_to_all(send_rows, "grp", split_axis=0, concat_axis=0, tiled=True),
        lax.all_to_all(send_pos, "grp", split_axis=0, concat_axis=0, tiled=True),
    )
    recv_rows = recv_rows.reshape(grp_count * SEND_CAP, image_rows.shape[1])
    recv_pos = recv_pos.reshape(grp_count * SEND_CAP)
    position_hit = jnp.arange(tok_count, dtype=jnp.int32)[:, None] == recv_pos[None, :]
    placed = jnp.dot(
        position_hit.astype(jnp.bfloat16), recv_rows, preferred_element_type=jnp.float32
    ).astype(jnp.bfloat16)
    covered = jnp.any(position_hit, axis=1)
    prompt = jnp.where(covered[:, None], placed, text)
    token_normed = layer_norm(prompt)
    all_tokens, all_segments = (
        lax.all_gather(token_normed, "tp", axis=0, tiled=True),
        lax.all_gather(segments, "tp", axis=1, tiled=True),
    )
    heads_txt = attention_heads(all_tokens, txt_qkv, all_segments[0], True)
    own_text = lax.all_to_all(heads_txt, "tp", split_axis=0, concat_axis=1, tiled=True)
    return (prompt.astype(jnp.float32) + project_out(own_text, txt_out)).astype(jnp.bfloat16)


def solution(mesh):
    placed = (
        P(("grp", "tp"), None),
        P("grp", "tp"),
        P(None, "tp", None),
        P(None, "grp"),
        P("tp", None),
        P(("grp", "tp"), None),
        P(("grp", "tp")),
        P("grp", "tp"),
        P(None, "tp", None),
        P(None, "grp"),
    )
    return jax.shard_map(
        per_device, mesh=mesh, in_specs=placed, out_specs=P(("grp", "tp"), None), check_vma=False
    )
```

profile of v0, /device:TPU:1, one launch (start us, length us, event | category | flops | bytes accessed | tf_op | source)
XLA Modules:
  0.0 397.2 jit_solution(6746148892684774772)
XLA Ops:
  11.7 14.0 %all_gather.26 = s32[1,1024]{1,0:T(1,128)S(1)} all-gather(s32[1,128]{1,0:T(1,128)} %param.11), channel_id=1, replica_groups=mesh['grp'=64,'tp'=8] {'tp'}, dimensions={1}, use_global_device_ids=true | all-gather | bytes 4608 | tf_op jit(solution)/shard_map/all_gather | solution.py:87
  26.3 31.7 %all-gather.8.cloned.1.call-done = bf16[1024,1280]{1,0:T(8,128)(2,1)} async-done(((bf16[128,1280]{1,0:T(8,128)(2,1)}), bf16[1024,1280]{1,0:T(8,128)(2,1)}) %all-gather.8.cloned.1.call-update) | async-done | bytes 2621456 | tf_op jit(solution)/shard_map/all_gather | solution.py:86
  63.7 4.6 %fusion.79 = (f32[2,512]{1,0:T(2,128)S(1)}, f32[2,512,1024]{2,1,0:T(8,128)}) fusion(pred[512,1024]{1,0:T(8,128)(4,1)S(1)} %get-tuple-element.12, bf16[512,2,80]{0,2,1:T(8,128)(2,1)S(1)} %bitcast.111, bf16[1024,2,80]{0,2,1:T(8,128)(2,1)} %bitcast.132), kind=kOutput, calls=%fused_computation.131 | convolution fusion | flops 171967488 | bytes 5214208 | tf_op jit(solution)/shard_map/sub | solution.py:55
  68.3 4.6 %fusion.80 = (f32[2,512]{1,0:T(2,128)S(1)}, f32[2,512,1024]{2,1,0:T(8,128)}) fusion(pred[512,1024]{1,0:T(8,128)(4,1)S(1)} %get-tuple-element.11, bf16[512,2,80]{0,2,1:T(8,128)(2,1)S(1)} %bitcast.109, bf16[1024,2,80]{0,2,1:T(8,128)(2,1)} %bitcast.133), kind=kOutput, calls=%fused_computation.132 | convolution fusion | flops 171967488 | bytes 5214208 | tf_op jit(solution)/shard_map/sub | solution.py:55
  73.0 3.2 fusion.27
  78.1 4.0 %all-to-all-start.1 = ((bf16[8,128,160]{1,2,0:T(8,128)(2,1)}), bf16[8,128,160]{1,2,0:T(8,128)(2,1)S(1)}, u32[]{:S(2)}, u32[]{:S(2)}) async-start(bf16[8,128,160]{1,2,0:T(8,128)(2,1)} %copy_bitcast_fusion.1), calls=%async_computation.1 | async-start | bytes 655360 | tf_op jit(solution)/shard_map/all_to_all | solution.py:90
  82.1 66.2 %all-gather.14.cloned.1.call-done = bf16[64,20,1280]{2,1,0:T(8,128)(2,1)} async-done(((bf16[1,20,1280]{2,1,0:T(8,128)(2,1)}), bf16[64,20,1280]{2,1,0:T(8,128)(2,1)}) %all-gather.14.cloned.1.call-update) | async-done | bytes 3276816 | tf_op jit(solution)/shard_map/all_gather | solution.py:74
  148.4 6.1 %reshape.296 = bf16[1280,1280]{1,0:T(8,128)(2,1)} reshape(bf16[64,20,1280]{2,1,0:T(8,128)(2,1)} %all-gather.14.cloned.1.call-done) | data formatting | bytes 6553600
  154.5 3.2 fusion.81
  159.4 37.7 %all-gather.10.cloned.1.call-done = bf16[256,5120]{1,0:T(8,128)(2,1)} async-done(((bf16[32,5120]{1,0:T(8,128)(2,1)}), bf16[256,5120]{1,0:T(8,128)(2,1)}) %all-gather.10.cloned.1.call-update) | async-done | bytes 2621456 | tf_op jit(solution)/shard_map/all_gather | solution.py:95
  200.7 4.0 %all-to-all-start.2 = ((bf16[8,32,160]{2,1,0:T(8,128)(2,1)}), bf16[8,32,160]{2,1,0:T(8,128)(2,1)S(1)}, u32[]{:S(2)}, u32[]{:S(2)}) async-start(bf16[8,32,160]{2,1,0:T(8,128)(2,1)} %bitcast.19), calls=%async_computation.2 | async-start | bytes 262144 | tf_op jit(solution)/shard_map/all_to_all | solution.py:98
  205.5 7.2 %all-to-all-done.2 = bf16[8,32,160]{2,1,0:T(8,128)(2,1)S(1)} async-done(((bf16[8,32,160]{2,1,0:T(8,128)(2,1)}), bf16[8,32,160]{2,1,0:T(8,128)(2,1)S(1)}, u32[]{:S(2)}, u32[]{:S(2)}) %all-to-all-start.2) | async-done | bytes 81952 | tf_op jit(solution)/shard_map/all_to_all | solution.py:98
  212.6 15.5 %all-to-all-start = ((s32[64,1,2]{2,1,0:T(1,128)}), s32[64,1,2]{2,1,0:T(1,128)S(1)}, u32[]{:S(2)}, u32[]{:S(2)}) async-start(s32[64,1,2]{2,1,0:T(1,128)} %bitcast), calls=%async_computation | async-start | bytes 65536 | tf_op jit(solution)/shard_map/all_to_all | solution.py:119
  229.6 7.8 %all-to-all-done = s32[64,1,2]{2,1,0:T(1,128)S(1)} async-done(((s32[64,1,2]{2,1,0:T(1,128)}), s32[64,1,2]{2,1,0:T(1,128)S(1)}, u32[]{:S(2)}, u32[]{:S(2)}) %all-to-all-start) | async-done | bytes 544 | tf_op jit(solution)/shard_map/all_to_all | solution.py:119
  237.5 4.9 %all-to-all-start.3 = ((bf16[64,2,1280]{2,1,0:T(2,128)(2,1)}), bf16[64,2,1280]{2,1,0:T(2,128)(2,1)S(1)}, u32[]{:S(2)}, u32[]{:S(2)}) async-start(bf16[64,2,1280]{2,1,0:T(2,128)(2,1)} %reshape.289), calls=%async_computation.3 | async-start | bytes 655360 | tf_op jit(solution)/shard_map/all_to_all | solution.py:118
  244.1 11.7 %all-to-all-done.3 = bf16[64,2,1280]{2,1,0:T(2,128)(2,1)S(1)} async-done(((bf16[64,2,1280]{2,1,0:T(2,128)(2,1)}), bf16[64,2,1280]{2,1,0:T(2,128)(2,1)S(1)}, u32[]{:S(2)}, u32[]{:S(2)}) %all-to-all-start.3) | async-done | bytes 327712 | tf_op jit(solution)/shard_map/all_to_all | solution.py:118
  258.0 10.6 %all_gather.31 = s32[1,1024]{1,0:T(1,128)S(1)} all-gather(s32[1,128]{1,0:T(1,128)S(1)} %copy-done.6), channel_id=1, replica_groups=mesh['grp'=64,'tp'=8] {'tp'}, dimensions={1}, use_global_device_ids=true | all-gather | bytes 4608 | tf_op jit(solution)/shard_map/all_gather | solution.py:132
  269.4 21.1 %all-gather.12.cloned.1.call-done = bf16[1024,1280]{1,0:T(8,128)(2,1)} async-done(((bf16[128,1280]{1,0:T(8,128)(2,1)}), bf16[1024,1280]{1,0:T(8,128)(2,1)}) %all-gather.12.cloned.1.call-update) | async-done | bytes 2621456 | tf_op jit(solution)/shard_map/all_gather | solution.py:131
  301.3 4.6 %fusion.83 = (f32[2,512]{1,0:T(2,128)S(1)}, f32[2,512,1024]{2,1,0:T(8,128)}) fusion(pred[512,1024]{1,0:T(8,128)(4,1)S(1)} %fusion.18, bf16[512,2,80]{0,2,1:T(8,128)(2,1)S(1)} %bitcast.110, bf16[1024,2,80]{0,2,1:T(8,128)(2,1)} %bitcast.121), kind=kOutput, calls=%fused_computation.135 | convolution fusion | flops 171967488 | bytes 5214208 | tf_op jit(solution)/shard_map/sub | solution.py:55
  305.9 3.1 fusion.26
  309.8 4.0 all-to-all-start.4
  313.8 66.9 %all-gather.16.cloned.1.call-done = bf16[64,20,1280]{2,1,0:T(8,128)(2,1)} async-done(((bf16[1,20,1280]{2,1,0:T(8,128)(2,1)}), bf16[64,20,1280]{2,1,0:T(8,128)(2,1)}) %all-gather.16.cloned.1.call-update) | async-done | bytes 3276816 | tf_op jit(solution)/shard_map/all_gather | solution.py:74
  380.7 6.1 %reshape.298 = bf16[1280,1280]{1,0:T(8,128)(2,1)} reshape(bf16[64,20,1280]{2,1,0:T(8,128)(2,1)} %all-gather.16.cloned.1.call-done) | data formatting | bytes 6553600
  386.8 3.9 fusion.8
  (91 shorter events, 36.8 us)
Async XLA Ops:
  6.5 190.6 %copy-start = (bf16[160,5120]{1,0:T(8,128)(2,1)S(1)}, bf16[160,5120]{1,0:T(8,128)(2,1)}, u32[]{:S(2)}) copy-start(bf16[160,5120]{1,0:T(8,128)(2,1)} %param.14) | copy-start | bytes 4915204
  6.5 51.5 %all-gather.8.cloned.1.call-start = ((), (), s32[]{:S(2)}) async-start(), calls=%async_computation.5 | async-start | bytes 2949120 | tf_op jit(solution)/shard_map/all_gather | solution.py:86
  10.9 137.5 %all-gather.14.cloned.1.call-start = ((), (), s32[]{:S(2)}) async-start(), calls=%async_computation.8 | async-start | bytes 3993600 | tf_op jit(solution)/shard_map/all_gather | solution.py:74
  58.0 3.0 copy-start.7
  58.0 3.0 copy-start.9
  73.0 3.4 copy-start.12
  78.1 76.4 %all-to-all-start.1 = ((bf16[8,128,160]{1,2,0:T(8,128)(2,1)}), bf16[8,128,160]{1,2,0:T(8,128)(2,1)S(1)}, u32[]{:S(2)}, u32[]{:S(2)}) async-start(bf16[8,128,160]{1,2,0:T(8,128)(2,1)} %copy_bitcast_fusion.1), calls=%async_computation.1 | async-start | bytes 655360 | tf_op jit(solution)/shard_map/all_to_all | solution.py:90
  82.1 72.4 %copy-start.1 = (bf16[128,1280]{1,0:T(8,128)(2,1)S(1)}, bf16[128,1280]{1,0:T(8,128)(2,1)}, u32[]{:S(2)}) copy-start(bf16[128,1280]{1,0:T(8,128)(2,1)} %param.10) | copy-start | bytes 983044
  82.1 115.1 %all-gather.10.cloned.1.call-start = ((), (), s32[]{:S(2)}) async-start(), calls=%async_computation.6 | async-start | bytes 2949120 | tf_op jit(solution)/shard_map/all_gather | solution.py:95
  154.5 4.6 %copy-start.11 = (s32[32]{0:T(128)S(1)}, s32[32]{0:T(128)}, u32[]{:S(2)}) copy-start(s32[32]{0:T(128)} %param.16) | copy-start | bytes 388
  199.9 56.0 %copy-start.2 = (bf16[128,1280]{1,0:T(8,128)(2,1)S(1)}, bf16[128,1280]{1,0:T(8,128)(2,1)}, u32[]{:S(2)}) copy-start(bf16[128,1280]{1,0:T(8,128)(2,1)} %param.15) | copy-start | bytes 983044
  200.7 12.0 %all-to-all-start.2 = ((bf16[8,32,160]{2,1,0:T(8,128)(2,1)}), bf16[8,32,160]{2,1,0:T(8,128)(2,1)S(1)}, u32[]{:S(2)}, u32[]{:S(2)}) async-start(bf16[8,32,160]{2,1,0:T(8,128)(2,1)} %bitcast.19), calls=%async_computation.2 | async-start | bytes 262144 | tf_op jit(solution)/shard_map/all_to_all | solution.py:98
  212.6 24.8 %all-to-all-start = ((s32[64,1,2]{2,1,0:T(1,128)}), s32[64,1,2]{2,1,0:T(1,128)S(1)}, u32[]{:S(2)}, u32[]{:S(2)}) async-start(s32[64,1,2]{2,1,0:T(1,128)} %bitcast), calls=%async_computation | async-start | bytes 65536 | tf_op jit(solution)/shard_map/all_to_all | solution.py:119
  228.8 29.2 %copy-start.6 = (s32[1,128]{1,0:T(1,128)S(1)}, s32[1,128]{1,0:T(1,128)}, u32[]{:S(2)}) copy-start(s32[1,128]{1,0:T(1,128)} %param.17) | copy-start | bytes 1540
  237.5 18.3 %all-to-all-start.3 = ((bf16[64,2,1280]{2,1,0:T(2,128)(2,1)}), bf16[64,2,1280]{2,1,0:T(2,128)(2,1)S(1)}, u32[]{:S(2)}, u32[]{:S(2)}) async-start(bf16[64,2,1280]{2,1,0:T(2,128)(2,1)} %reshape.289), calls=%async_computation.3 | async-start | bytes 655360 | tf_op jit(solution)/shard_map/all_to_all | solution.py:118
  242.4 48.1 %all-gather.12.cloned.1.call-start = ((), (), s32[]{:S(2)}) async-start(), calls=%async_computation.7 | async-start | bytes 2949120 | tf_op jit(solution)/shard_map/all_gather | solution.py:131
  257.4 123.4 %all-gather.16.cloned.1.call-start = ((), (), s32[]{:S(2)}) async-start(), calls=%async_computation.9 | async-start | bytes 3993600 | tf_op jit(solution)/shard_map/all_gather | solution.py:74
  290.5 3.7 copy-start.8
  290.5 3.7 copy-start.10
  293.4 1.7 copy-start.4
  295.2 1.7 copy-start.5
  297.0 2.0 copy-start.3
  309.8 77.0 %all-to-all-start.4 = ((bf16[8,128,160]{1,2,0:T(8,128)(2,1)}), bf16[8,128,160]{1,2,0:T(8,128)(2,1)S(1)}, u32[]{:S(2)}, u32[]{:S(2)}) async-start(bf16[8,128,160]{1,2,0:T(8,128)(2,1)} %copy_bitcast_fusion), calls=%async_computation.4 | async-start | bytes 655360 | tf_op jit(solution)/shard_map/all_to_all | solution.py:135
Sparse Core Ops, SparseCore 0:
  11.0 46.9 all-gather.7
  61.3 87.0 all-gather.13
  159.2 37.8 all-gather.9
  257.5 32.9 all-gather.11
  293.6 87.0 all-gather.15
where the time goes:
time: 398 us; the launch traced here: 397 us
  waiting for transfers between devices  252 us (63%)
  matrix products  46.3 us (12%)
  starting transfers between devices  32.6 us (8%)
  blocking collectives  24.6 us (6%)
  local copies, waits for them, and re-layouts  18.4 us (5%)
  between operations  13.5 us (3%)
  other arithmetic  10 us (3%)
    all_gather x2, waiting for transfers between devices, project_out(): lax.all_gather(columns, 'grp', axis=1, tiled=True)  133 us
    all_gather x1, waiting for transfers between devices, per_device(): lax.all_gather(merged, 'tp', axis=0, tiled=True)  37.7 us
    all_gather x1, waiting for transfers between devices, per_device(): lax.all_gather(patch_normed, 'tp', axis=0, tiled=True)  31.7 us
    all_gather x1, waiting for transfers between devices, per_device(): lax.all_gather(token_normed, 'tp', axis=0, tiled=True)  21.1 us
    sub x4, matrix products, local_attention(): weights = jnp.exp(scores - row_max)  15.8 us
    all_to_all x1, starting transfers between devices, per_device(): lax.all_to_all(send_pos, 'grp', split_axis=0, concat_axis=0, tiled=True)  15.5 us
    all_gather x1, blocking collectives, per_device(): lax.all_gather(pictures, 'tp', axis=1, tiled=True)  14 us
    dot_general x7, matrix products, times_transpose(): lax.dot_general(left, right, (((1,), (1,)), ((), ())), preferred_element_...  13.3 us
  transfers between devices with their start and end apart: 10, of which 8 were waited for; matrix products, arithmetic and copies ran while one was open for 14% of the time, Pallas kernels for 0%

commit v1 on v0

--- a/solution.py
+++ b/solution.py
@@ -127,8 +127,11 @@
     covered = jnp.any(position_hit, axis=1)
     prompt = jnp.where(covered[:, None], placed, text)
     token_normed = layer_norm(prompt)
+    view_rates = lambda mine_x, ndim_at: jnp.concatenate(
+        lax.all_to_all(jnp.stack(lax.axis_size("tp") * [mine_x], axis=0), "tp", 0, 0), ndim_at
+    )
     all_tokens, all_segments = (
-        lax.all_gather(token_normed, "tp", axis=0, tiled=True),
+        view_rates(token_normed, 0),
         lax.all_gather(segments, "tp", axis=1, tiled=True),
     )
     heads_txt = attention_heads(all_tokens, txt_qkv, all_segments[0], True)

time: 398 us -> 383 us (0.962)
  waiting for transfers between devices: 252 us -> 168 us
  blocking collectives: 24.6 us -> 80.9 us
  starting transfers between devices: 32.6 us -> 37.8 us
    all_gather x2, waiting for transfers between devices: 133 us -> 66.3 us  [project_out(): lax.all_gather(columns, 'grp', axis=1, tiled=True)]
    all_gather x1, blocking collectives: 10.6 us -> 66.9 us  [per_device(): lax.all_gather(segments, 'tp', axis=1, tiled=True)]
    all_gather x1 -> x0, waiting for transfers between devices: 21.1 us -> none  [per_device(): lax.all_gather(token_normed, 'tp', axis=0, tiled=True)]
    all_to_all x0 -> x1, starting transfers between devices: none -> 4.51 us  [per_device(): lax.all_to_all(jnp.stack(lax.axis_size('tp') * [mine_x], axis=0), 'tp', 0...]
    all_to_all x1, waiting for transfers between devices: 0.01 us -> 4.18 us  [per_device(): lax.all_to_all(heads_txt, 'tp', split_axis=0, concat_axis=1, tiled=True)]
    unnamed x28 -> x26, local copies, waits for them, and re-layouts: 12.6 us -> 12.6 us
  transfers between devices with their start and end apart: 10 -> 10, of which waited for: 8 -> 7; matrix products, arithmetic and copies ran while one was open for 14% -> 16% of each run, Pallas kernels for 0% -> 0%
where the time goes in v1:
time: 383 us; the launch traced here: 379 us
  waiting for transfers between devices  168 us (44%)
  blocking collectives  80.9 us (21%)
  matrix products  49.9 us (13%)
  starting transfers between devices  37.8 us (10%)
  local copies, waits for them, and re-layouts  20.2 us (5%)
  between operations  13.5 us (4%)
  other arithmetic  9.3 us (2%)
    all_gather x1, blocking collectives, per_device(): lax.all_gather(segments, 'tp', axis=1, tiled=True)  66.9 us
    all_gather x2, waiting for transfers between devices, project_out(): lax.all_gather(columns, 'grp', axis=1, tiled=True)  66.3 us
    all_gather x1, waiting for transfers between devices, per_device(): lax.all_gather(merged, 'tp', axis=0, tiled=True)  37.7 us
    all_gather x1, waiting for transfers between devices, per_device(): lax.all_gather(patch_normed, 'tp', axis=0, tiled=True)  31.7 us
    dot_general x7, matrix products, times_transpose(): lax.dot_general(left, right, (((1,), (1,)), ((), ())), preferred_element_...  16.9 us
    sub x4, matrix products, local_attention(): weights = jnp.exp(scores - row_max)  15.8 us
    all_to_all x1, starting transfers between devices, per_device(): lax.all_to_all(send_pos, 'grp', split_axis=0, concat_axis=0, tiled=True)  15.5 us
    all_gather x1, blocking collectives, per_device(): lax.all_gather(pictures, 'tp', axis=1, tiled=True)  14 us
  transfers between devices with their start and end apart: 10, of which 7 were waited for; matrix products, arithmetic and copies ran while one was open for 16% of the time, Pallas kernels for 0%

profile of v1, /device:TPU:1, one launch (start us, length us, event | category | flops | bytes accessed | tf_op | source)
XLA Modules:
  0.0 379.4 jit_solution(4563801953519058728)
XLA Ops:
  11.7 14.0 %all_gather.23 = s32[1,1024]{1,0:T(1,128)S(1)} all-gather(s32[1,128]{1,0:T(1,128)} %param.11), channel_id=1, replica_groups=mesh['grp'=64,'tp'=8] {'tp'}, dimensions={1}, use_global_device_ids=true | all-gather | bytes 4608 | tf_op jit(solution)/shard_map/all_gather | solution.py:87
  26.3 31.7 %all-gather.7.cloned.1.call-done = bf16[1024,1280]{1,0:T(8,128)(2,1)} async-done(((bf16[128,1280]{1,0:T(8,128)(2,1)}), bf16[1024,1280]{1,0:T(8,128)(2,1)}) %all-gather.7.cloned.1.call-update) | async-done | bytes 2621456 | tf_op jit(solution)/shard_map/all_gather | solution.py:86
  63.7 4.6 %fusion.79 = (f32[2,512]{1,0:T(2,128)S(1)}, f32[2,512,1024]{2,1,0:T(8,128)}) fusion(pred[512,1024]{1,0:T(8,128)(4,1)S(1)} %get-tuple-element.12, bf16[512,2,80]{0,2,1:T(8,128)(2,1)S(1)} %bitcast.112, bf16[1024,2,80]{0,2,1:T(8,128)(2,1)} %bitcast.133), kind=kOutput, calls=%fused_computation.131 | convolution fusion | flops 171967488 | bytes 5214208 | tf_op jit(solution)/shard_map/sub | solution.py:55
  68.3 4.6 %fusion.80 = (f32[2,512]{1,0:T(2,128)S(1)}, f32[2,512,1024]{2,1,0:T(8,128)}) fusion(pred[512,1024]{1,0:T(8,128)(4,1)S(1)} %get-tuple-element.11, bf16[512,2,80]{0,2,1:T(8,128)(2,1)S(1)} %bitcast.110, bf16[1024,2,80]{0,2,1:T(8,128)(2,1)} %bitcast.134), kind=kOutput, calls=%fused_computation.132 | convolution fusion | flops 171967488 | bytes 5214208 | tf_op jit(solution)/shard_map/sub | solution.py:55
  73.0 3.2 fusion.27
  78.1 4.0 %all-to-all-start.1 = ((bf16[8,128,160]{1,2,0:T(8,128)(2,1)}), bf16[8,128,160]{1,2,0:T(8,128)(2,1)S(1)}, u32[]{:S(2)}, u32[]{:S(2)}) async-start(bf16[8,128,160]{1,2,0:T(8,128)(2,1)} %copy_bitcast_fusion.1), calls=%async_computation.1 | async-start | bytes 655360 | tf_op jit(solution)/shard_map/all_to_all | solution.py:90
  82.1 66.2 %all-gather.11.cloned.1.call-done = bf16[64,20,1280]{2,1,0:T(8,128)(2,1)} async-done(((bf16[1,20,1280]{2,1,0:T(8,128)(2,1)}), bf16[64,20,1280]{2,1,0:T(8,128)(2,1)}) %all-gather.11.cloned.1.call-update) | async-done | bytes 3276816 | tf_op jit(solution)/shard_map/all_gather | solution.py:74
  148.4 6.1 %reshape.302 = bf16[1280,1280]{1,0:T(8,128)(2,1)} reshape(bf16[64,20,1280]{2,1,0:T(8,128)(2,1)} %all-gather.11.cloned.1.call-done) | data formatting | bytes 6553600
  154.5 3.2 fusion.81
  159.4 37.7 %all-gather.9.cloned.1.call-done = bf16[256,5120]{1,0:T(8,128)(2,1)} async-done(((bf16[32,5120]{1,0:T(8,128)(2,1)}), bf16[256,5120]{1,0:T(8,128)(2,1)}) %all-gather.9.cloned.1.call-update) | async-done | bytes 2621456 | tf_op jit(solution)/shard_map/all_gather | solution.py:95
  200.7 4.0 %all-to-all-start.2 = ((bf16[8,32,160]{2,1,0:T(8,128)(2,1)}), bf16[8,32,160]{2,1,0:T(8,128)(2,1)S(1)}, u32[]{:S(2)}, u32[]{:S(2)}) async-start(bf16[8,32,160]{2,1,0:T(8,128)(2,1)} %bitcast.19), calls=%async_computation.2 | async-start | bytes 262144 | tf_op jit(solution)/shard_map/all_to_all | solution.py:98
  205.5 7.2 %all-to-all-done.2 = bf16[8,32,160]{2,1,0:T(8,128)(2,1)S(1)} async-done(((bf16[8,32,160]{2,1,0:T(8,128)(2,1)}), bf16[8,32,160]{2,1,0:T(8,128)(2,1)S(1)}, u32[]{:S(2)}, u32[]{:S(2)}) %all-to-all-start.2) | async-done | bytes 81952 | tf_op jit(solution)/shard_map/all_to_all | solution.py:98
  212.6 15.5 %all-to-all-start = ((s32[64,1,2]{2,1,0:T(1,128)}), s32[64,1,2]{2,1,0:T(1,128)S(1)}, u32[]{:S(2)}, u32[]{:S(2)}) async-start(s32[64,1,2]{2,1,0:T(1,128)} %bitcast), calls=%async_computation | async-start | bytes 65536 | tf_op jit(solution)/shard_map/all_to_all | solution.py:119
  229.6 7.8 %all-to-all-done = s32[64,1,2]{2,1,0:T(1,128)S(1)} async-done(((s32[64,1,2]{2,1,0:T(1,128)}), s32[64,1,2]{2,1,0:T(1,128)S(1)}, u32[]{:S(2)}, u32[]{:S(2)}) %all-to-all-start) | async-done | bytes 544 | tf_op jit(solution)/shard_map/all_to_all | solution.py:119
  237.5 4.9 %all-to-all-start.3 = ((bf16[64,2,1280]{2,1,0:T(2,128)(2,1)}), bf16[64,2,1280]{2,1,0:T(2,128)(2,1)S(1)}, u32[]{:S(2)}, u32[]{:S(2)}) async-start(bf16[64,2,1280]{2,1,0:T(2,128)(2,1)} %reshape.294), calls=%async_computation.3 | async-start | bytes 655360 | tf_op jit(solution)/shard_map/all_to_all | solution.py:118
  244.0 11.7 %all-to-all-done.3 = bf16[64,2,1280]{2,1,0:T(2,128)(2,1)S(1)} async-done(((bf16[64,2,1280]{2,1,0:T(2,128)(2,1)}), bf16[64,2,1280]{2,1,0:T(2,128)(2,1)S(1)}, u32[]{:S(2)}, u32[]{:S(2)}) %all-to-all-start.3) | async-done | bytes 327712 | tf_op jit(solution)/shard_map/all_to_all | solution.py:118
  258.3 4.5 %all-to-all-start.4 = ((bf16[8,128,1280]{2,1,0:T(8,128)(2,1)}), bf16[8,128,1280]{2,1,0:T(8,128)(2,1)}, u32[]{:S(2)}, u32[]{:S(2)}) async-start(bf16[8,128,1280]{2,1,0:T(8,128)(2,1)} %stack.2), calls=%async_computation.4 | async-start | bytes 5242880 | tf_op jit(solution)/shard_map/all_to_all | solution.py:131
  263.4 66.9 %all_gather.27 = s32[1,1024]{1,0:T(1,128)S(1)} all-gather(s32[1,128]{1,0:T(1,128)S(1)} %copy-done.6), channel_id=1, replica_groups=mesh['grp'=64,'tp'=8] {'tp'}, dimensions={1}, use_global_device_ids=true | all-gather | bytes 4608 | tf_op jit(solution)/shard_map/all_gather | solution.py:135
  345.5 4.6 %fusion.83 = (f32[2,512]{1,0:T(2,128)S(1)}, f32[2,512,1024]{2,1,0:T(8,128)}) fusion(pred[512,1024]{1,0:T(8,128)(4,1)S(1)} %fusion.18, bf16[512,2,80]{0,2,1:T(8,128)(2,1)S(1)} %bitcast.111, bf16[1024,2,80]{0,2,1:T(8,128)(2,1)} %bitcast.122), kind=kOutput, calls=%fused_computation.135 | convolution fusion | flops 171967488 | bytes 5214208 | tf_op jit(solution)/shard_map/sub | solution.py:55
  350.1 3.1 fusion.26
  354.0 4.7 %all-to-all-start.5 = ((bf16[8,128,160]{1,2,0:T(8,128)(2,1)}), bf16[8,128,160]{1,2,0:T(8,128)(2,1)S(1)}, u32[]{:S(2)}, u32[]{:S(2)}) async-start(bf16[8,128,160]{1,2,0:T(8,128)(2,1)} %copy_bitcast_fusion), calls=%async_computation.5 | async-start | bytes 655360 | tf_op jit(solution)/shard_map/all_to_all | solution.py:138
  358.7 6.1 %reshape.304 = bf16[1280,1280]{1,0:T(8,128)(2,1)} reshape(bf16[64,20,1280]{2,1,0:T(8,128)(2,1)} %all-gather.13.cloned.1.call-done) | data formatting | bytes 6553600
  364.8 4.2 %all-to-all-done.5 = bf16[8,128,160]{1,2,0:T(8,128)(2,1)S(1)} async-done(((bf16[8,128,160]{1,2,0:T(8,128)(2,1)}), bf16[8,128,160]{1,2,0:T(8,128)(2,1)S(1)}, u32[]{:S(2)}, u32[]{:S(2)}) %all-to-all-start.5) | async-done | bytes 327712 | tf_op jit(solution)/shard_map/all_to_all | solution.py:138
  369.0 3.9 %fusion.8 = bf16[128,1280]{1,0:T(8,128)(2,1)} fusion(f32[128,1280]{1,0:T(8,128)S(1)} %get-tuple-element.24, bf16[128,1280]{0,1:T(8,128)(2,1)S(1)} %bitcast.107, bf16[1280,1280]{1,0:T(8,128)(2,1)} %reshape.304), kind=kOutput, calls=%fused_computation.19 | convolution fusion | flops 419758080 | bytes 4587520 | tf_op jit(solution)/shard_map/dot_general | solution.py:72
  (89 shorter events, 41.3 us)
Async XLA Ops:
  6.5 190.6 %copy-start = (bf16[160,5120]{1,0:T(8,128)(2,1)S(1)}, bf16[160,5120]{1,0:T(8,128)(2,1)}, u32[]{:S(2)}) copy-start(bf16[160,5120]{1,0:T(8,128)(2,1)} %param.14) | copy-start | bytes 4915204
  6.5 51.5 %all-gather.7.cloned.1.call-start = ((), (), s32[]{:S(2)}) async-start(), calls=%async_computation.6 | async-start | bytes 2949120 | tf_op jit(solution)/shard_map/all_gather | solution.py:86
  10.9 137.5 %all-gather.11.cloned.1.call-start = ((), (), s32[]{:S(2)}) async-start(), calls=%async_computation.8 | async-start | bytes 3993600 | tf_op jit(solution)/shard_map/all_gather | solution.py:74
  58.0 3.0 copy-start.7
  58.0 3.0 copy-start.8
  73.0 3.4 copy-start.11
  78.1 76.4 %all-to-all-start.1 = ((bf16[8,128,160]{1,2,0:T(8,128)(2,1)}), bf16[8,128,160]{1,2,0:T(8,128)(2,1)S(1)}, u32[]{:S(2)}, u32[]{:S(2)}) async-start(bf16[8,128,160]{1,2,0:T(8,128)(2,1)} %copy_bitcast_fusion.1), calls=%async_computation.1 | async-start | bytes 655360 | tf_op jit(solution)/shard_map/all_to_all | solution.py:90
  82.1 72.4 %copy-start.1 = (bf16[128,1280]{1,0:T(8,128)(2,1)S(1)}, bf16[128,1280]{1,0:T(8,128)(2,1)}, u32[]{:S(2)}) copy-start(bf16[128,1280]{1,0:T(8,128)(2,1)} %param.10) | copy-start | bytes 983044
  82.1 115.1 %all-gather.9.cloned.1.call-start = ((), (), s32[]{:S(2)}) async-start(), calls=%async_computation.7 | async-start | bytes 2949120 | tf_op jit(solution)/shard_map/all_gather | solution.py:95
  154.5 4.6 %copy-start.10 = (s32[32]{0:T(128)S(1)}, s32[32]{0:T(128)}, u32[]{:S(2)}) copy-start(s32[32]{0:T(128)} %param.16) | copy-start | bytes 388
  199.9 56.0 %copy-start.2 = (bf16[128,1280]{1,0:T(8,128)(2,1)S(1)}, bf16[128,1280]{1,0:T(8,128)(2,1)}, u32[]{:S(2)}) copy-start(bf16[128,1280]{1,0:T(8,128)(2,1)} %param.15) | copy-start | bytes 983044
  200.7 12.0 %all-to-all-start.2 = ((bf16[8,32,160]{2,1,0:T(8,128)(2,1)}), bf16[8,32,160]{2,1,0:T(8,128)(2,1)S(1)}, u32[]{:S(2)}, u32[]{:S(2)}) async-start(bf16[8,32,160]{2,1,0:T(8,128)(2,1)} %bitcast.19), calls=%async_computation.2 | async-start | bytes 262144 | tf_op jit(solution)/shard_map/all_to_all | solution.py:98
  212.6 24.8 %all-to-all-start = ((s32[64,1,2]{2,1,0:T(1,128)}), s32[64,1,2]{2,1,0:T(1,128)S(1)}, u32[]{:S(2)}, u32[]{:S(2)}) async-start(s32[64,1,2]{2,1,0:T(1,128)} %bitcast), calls=%async_computation | async-start | bytes 65536 | tf_op jit(solution)/shard_map/all_to_all | solution.py:119
  237.5 18.3 %all-to-all-start.3 = ((bf16[64,2,1280]{2,1,0:T(2,128)(2,1)}), bf16[64,2,1280]{2,1,0:T(2,128)(2,1)S(1)}, u32[]{:S(2)}, u32[]{:S(2)}) async-start(bf16[64,2,1280]{2,1,0:T(2,128)(2,1)} %reshape.294), calls=%async_computation.3 | async-start | bytes 655360 | tf_op jit(solution)/shard_map/all_to_all | solution.py:118
  258.3 5.1 %copy-start.6 = (s32[1,128]{1,0:T(1,128)S(1)}, s32[1,128]{1,0:T(1,128)}, u32[]{:S(2)}) copy-start(s32[1,128]{1,0:T(1,128)} %param.17) | copy-start | bytes 1540
  258.3 72.8 %all-to-all-start.4 = ((bf16[8,128,1280]{2,1,0:T(8,128)(2,1)}), bf16[8,128,1280]{2,1,0:T(8,128)(2,1)}, u32[]{:S(2)}, u32[]{:S(2)}) async-start(bf16[8,128,1280]{2,1,0:T(8,128)(2,1)} %stack.2), calls=%async_computation.4 | async-start | bytes 5242880 | tf_op jit(solution)/shard_map/all_to_all | solution.py:131
  262.9 95.8 %all-gather.13.cloned.1.call-start = ((), (), s32[]{:S(2)}) async-start(), calls=%async_computation.9 | async-start | bytes 3993600 | tf_op jit(solution)/shard_map/all_gather | solution.py:74
  331.2 3.7 copy-start.9
  334.1 3.5 copy-start.4
  337.6 3.5 copy-start.5
  341.2 2.0 copy-start.3
  354.0 15.0 %all-to-all-start.5 = ((bf16[8,128,160]{1,2,0:T(8,128)(2,1)}), bf16[8,128,160]{1,2,0:T(8,128)(2,1)S(1)}, u32[]{:S(2)}, u32[]{:S(2)}) async-start(bf16[8,128,160]{1,2,0:T(8,128)(2,1)} %copy_bitcast_fusion), calls=%async_computation.5 | async-start | bytes 655360 | tf_op jit(solution)/shard_map/all_to_all | solution.py:138
Sparse Core Ops, SparseCore 0:
  11.0 46.9 all-gather.6
  61.3 87.0 all-gather.10
  159.2 37.8 all-gather.8
  266.6 82.2 all-gather.12
